TPU v7x, 32 devices: a whole 2x2x4 slice. The times are simulated.
32 devices in a mesh: segment: 4 (over y, x), seq: 8 (over z, core).
Axes of the slice: x: 2, y: 2, z: 4, core: 2. Of those that a mesh axis runs over, the one named last changes fastest.
Arguments:
- hidden: bfloat16 [4, 8192, 8192], P('segment', 'seq'), may hold values from -6 to 6
- span_lengths: int32 [4, 64], replicated, may hold values from 1 to 512, 8192 in all within a row
- section_of: int32 [4, 64], replicated, may hold values from 0 to 31
- section_live: int32 [32], P('seq'), may hold values 0 or 1
- w_in: bfloat16 [8192, 2048], P('seq'), may hold values from -0.5 to 0.5
- norm_gain: float32 [2048], replicated, may hold values from 0.5 to 1.5
- w_query: bfloat16 [2048, 2048], P(None, 'segment'), may hold values from -0.125 to 0.125
- w_key: bfloat16 [2048, 2048], P(None, 'segment'), may hold values from -0.125 to 0.125
- w_value: bfloat16 [2048, 2048], P(None, 'segment'), may hold values from -0.125 to 0.125
- w_out: bfloat16 [2048, 2048], P('segment'), may hold values from -0.125 to 0.125
Outputs:
- section_out: bfloat16 [32, 2048], P('seq')
All inputs are finite; a program needn't handle non-finite values. No bound on the sum of `section_live` on one device may be relied on, other than what follows from the above.
Results may differ from a plain program's by a relative error of at most 0.007.
Values may be sent and summed in bfloat16 or wider, within the bound.
A program may use at most 128 MiB of HBM per device.

v0:
```python
import jax
import jax.numpy as jnp
from jax import lax
from jax.sharding import PartitionSpec as P

HEAD_DIM = 128


def shards(
    hidden, span_lengths, section_of, section_live, w_in, norm_gain, w_query, w_key, w_value, w_out
):
    tokens = hidden[0]
    seq_count = lax.axis_size("seq")
    seq_index = lax.axis_index("seq")
    segment_index = lax.axis_index("segment")
    tok_count = tokens.shape[0]
    lengths = lax.dynamic_index_in_dim(span_lengths, segment_index, 0, keepdims=False)
    span_ends = jnp.cumsum(lengths)
    span_starts = span_ends - lengths
    positions = seq_index * tok_count + jnp.arange(tok_count, dtype=jnp.int32)
    member = (
        (positions[None, :] >= span_starts[:, None]) & (positions[None, :] < span_ends[:, None])
    ).astype(jnp.bfloat16)
    partial_value = jnp.dot(member, tokens, preferred_element_type=jnp.float32)
    length_float = lengths.astype(jnp.float32)
    sections_here = section_live.shape[0]
    section_total = sections_here * seq_count
    section_ids = jnp.arange(section_total, dtype=jnp.int32)
    own_sections = seq_index * sections_here + jnp.arange(sections_here, dtype=jnp.int32)
    flat_sections = section_of.reshape(-1)
    count_all = jnp.sum(
        (section_ids[:, None] == flat_sections[None, :]).astype(jnp.float32), axis=1
    )
    doc_sections = lax.dynamic_index_in_dim(section_of, segment_index, 0, keepdims=False)
    weighted = partial_value / length_float[:, None]
    doc_onehot = (section_ids[:, None] == doc_sections[None, :]).astype(jnp.float32)
    section_part = jnp.dot(doc_onehot, weighted, precision=lax.Precision.HIGHEST)
    feature_block = lax.psum_scatter(section_part, "seq", scatter_dimension=1, tiled=True)
    doc_total = lax.psum(feature_block, "segment")
    pooled = (doc_total / jnp.maximum(count_all, 1.0)[:, None]).astype(jnp.bfloat16)
    projected = jnp.dot(pooled, w_in, preferred_element_type=jnp.float32)
    section_in = lax.psum_scatter(projected, "seq", scatter_dimension=0, tiled=True)
    scale = lax.rsqrt(jnp.mean(section_in * section_in, axis=1, keepdims=True) + 1e-05)
    normed = (section_in * scale * norm_gain[None, :]).astype(jnp.bfloat16)
    queries = jnp.dot(normed, w_query, preferred_element_type=jnp.float32).astype(jnp.bfloat16)
    keys_here = jnp.dot(normed, w_key, preferred_element_type=jnp.float32).astype(jnp.bfloat16)
    values_here = jnp.dot(normed, w_value, preferred_element_type=jnp.float32).astype(jnp.bfloat16)
    live_here = section_live.astype(jnp.bfloat16)
    keys_all, values_all, live_all = (
        lax.all_gather(keys_here, "seq", axis=0, tiled=True),
        lax.all_gather(values_here, "seq", axis=0, tiled=True),
        lax.all_gather(live_here, "seq", axis=0, tiled=True),
    )
    local_heads = queries.shape[1] // HEAD_DIM
    query_heads = queries.reshape(sections_here, local_heads, HEAD_DIM)
    key_heads = keys_all.reshape(section_total, local_heads, HEAD_DIM)
    value_heads = values_all.reshape(section_total, local_heads, HEAD_DIM)
    scores = jnp.einsum("qhd,khd->hqk", query_heads, key_heads, preferred_element_type=jnp.float32)
    scores = scores / jnp.sqrt(jnp.float32(HEAD_DIM))
    allowed = (live_all[None, :] > 0) | (section_ids[None, :] == own_sections[:, None])
    scores = jnp.where(allowed[None, :, :], scores, jnp.float32(-1e30))
    probs = jax.nn.softmax(scores, axis=-1).astype(jnp.bfloat16)
    attended = jnp.einsum(
        "hqk,khd->qhd", probs, value_heads, preferred_element_type=jnp.float32
    ).astype(jnp.bfloat16)
    attended = attended.reshape(sections_here, local_heads * HEAD_DIM)
    head_terms = jnp.dot(attended, w_out, preferred_element_type=jnp.float32)
    combined = lax.psum(head_terms, "segment")
    return (section_in + combined).astype(jnp.bfloat16)


def solution(mesh):
    in_specs = (
        P("segment", "seq", None),
        P(),
        P(),
        P("seq"),
        P("seq", None),
        P(),
        P(None, "segment"),
        P(None, "segment"),
        P(None, "segment"),
        P("segment", None),
    )
    out_specs = P("seq", None)
    return jax.shard_map(shards, mesh=mesh, in_specs=in_specs, out_specs=out_specs, check_vma=False)
```

profile of v0, /device:TPU:0, one launch (start us, length us, event | category | flops | bytes accessed | tf_op | source)
XLA Modules:
  0.0 217.7 jit_solution(10877947771555918930)
XLA Ops:
  6.5 0.9 fusion.30
  7.4 0.1 copy.25
  7.6 0.1 reduce
  7.7 0.7 bitcast_subtract_fusion
  8.4 8.8 %fusion.3 = f32[64,8192]{1,0:T(8,128)S(1)} fusion(bf16[1,1024,8192]{2,1,0:T(8,128)(2,1)} %param.10, f32[64]{0:T(128)S(1)} %get-tuple-element.6, s32[1024]{0:T(1024)S(1)} %iota_add_fusion, s32[64]{0:T(128)S(1)} %reduce, s32[64]{0:T(128)S(1)} %bitcast_subtract_fusion), kind=kOutput, calls=%fused_computation.3 | convolution fusion | flops 1074462720 | bytes 18879232 | tf_op jit(solution)/shard_map/dot_general | solution.py:24
  17.3 1.8 fusion.25
  19.3 0.7 fusion.31
  20.6 0.2 dynamic-update-slice
  20.9 18.2 %all-reduce = bf16[32]{0:T(256)(128)(2,1)S(1)} all-reduce(bf16[32]{0:T(256)(128)(2,1)S(1)} %dynamic-update-slice), channel_id=1, replica_groups=mesh['segment'=4,'seq'=8] {'seq'}, use_global_device_ids=true, to_apply=%add | all-reduce | flops 32 | bytes 128
  39.1 0.1 convert_reduce_fusion
  39.2 15.9 %reduce-scatter.2.cloned.1.call-done = f32[32,1024]{1,0:T(8,128)} async-done(((f32[32,8192]{1,0:T(8,128)}), f32[32,1024]{1,0:T(8,128)}) %reduce-scatter.2.cloned.1.call-update) | async-done | bytes 131088 | tf_op jit(solution)/shard_map/reduce_scatter | solution.py:38
  55.8 42.1 %all-reduce.5.cloned.1.call-done = f32[32,1024]{1,0:T(8,128)} async-done(((f32[32,1024]{1,0:T(8,128)}), f32[32,1024]{1,0:T(8,128)}) %all-reduce.5.cloned.1.call-update) | async-done | bytes 131088 | tf_op jit(solution)/shard_map/psum | solution.py:39
  97.9 3.8 %fusion.20 = f32[32,2048]{1,0:T(8,128)} fusion(bf16[1024,2048]{1,0:T(8,128)(2,1)} %param.14, f32[32,1024]{1,0:T(8,128)} %all-reduce.5.cloned.1.call-done, f32[32]{0:T(128)S(1)} %broadcast_maximum_fusion), kind=kOutput, calls=%fused_computation.24 | convolution fusion | flops 134283264 | bytes 4587648 | tf_op jit(solution)/shard_map/dot_general | solution.py:41
  101.8 55.5 %all-reduce.7.cloned.1.call-done = f32[32,2048]{1,0:T(8,128)} async-done(((f32[32,2048]{1,0:T(8,128)}), f32[32,2048]{1,0:T(8,128)}) %all-reduce.7.cloned.1.call-update) | async-done | bytes 262160
  157.3 1.0 multiply_reduce_fusion
  158.3 2.0 fusion.11
  160.3 14.1 %all-gather.1 = bf16[8,4,512]{2,1,0:T(4,128)(2,1)S(1)} all-gather(bf16[1,4,512]{2,1,0:T(4,128)(2,1)S(1)} %fusion.11), channel_id=1, replica_groups=mesh['segment'=4,'seq'=8] {'seq'}, dimensions={0}, use_global_device_ids=true | all-gather | bytes 36864 | tf_op jit(solution)/shard_map/all_gather | solution.py:50
  174.4 2.2 fusion.8
  176.6 0.2 fusion.32
  176.8 2.1 fusion.9
  178.8 14.1 %all-gather = bf16[8,4,512]{2,1,0:T(4,128)(2,1)S(1)} all-gather(bf16[1,4,512]{2,1,0:T(4,128)(2,1)S(1)} %fusion.9), channel_id=1, replica_groups=mesh['segment'=4,'seq'=8] {'seq'}, dimensions={0}, use_global_device_ids=true | all-gather | bytes 36864 | tf_op jit(solution)/shard_map/all_gather | solution.py:51
  193.0 0.5 fusion.13
  193.5 16.2 %psum.15 = f32[4,2048]{1,0:T(4,128)S(1)} all-reduce(f32[4,2048]{1,0:T(4,128)S(1)} %fusion.13), channel_id=1, replica_groups=mesh['segment'=4,'seq'=8] {'segment'}, use_global_device_ids=true, to_apply=%region_8.9 | all-reduce | flops 8192 | bytes 65536 | tf_op jit(solution)/shard_map/psum | solution.py:68
  209.7 1.5 add_convert_fusion
  (28 shorter events, 0.5 us)
Async XLA Ops:
  6.5 186.4 %copy-start = (bf16[512,2048]{1,0:T(8,128)(2,1)S(1)}, bf16[512,2048]{1,0:T(8,128)(2,1)}, u32[]{:S(2)}) copy-start(bf16[512,2048]{1,0:T(8,128)(2,1)} %param.19) | copy-start | bytes 6291460
  6.5 48.5 %reduce-scatter.2.cloned.1.call-start = ((), (), s32[]{:S(2)}) async-start(), calls=%async_computation.1 | async-start | bytes 1179648 | tf_op jit(solution)/shard_map/reduce_scatter | solution.py:38
  17.3 1.9 copy-start.2
  17.3 2.0 copy-start.4
  17.3 2.0 copy-start.3
  19.1 78.7 %all-reduce.5.cloned.1.call-start = ((), (), s32[]{:S(2)}) async-start(), calls=%async_computation.2 | async-start | bytes 262144 | tf_op jit(solution)/shard_map/psum | solution.py:39
  55.1 102.2 %all-reduce.7.cloned.1.call-start = ((), (), s32[]{:S(2)}) async-start(), calls=%async_computation.3 | async-start | bytes 524288
  55.8 102.5 %copy-start.1 = (f32[2048]{0:T(1024)S(1)}, f32[2048]{0:T(1024)}, u32[]{:S(2)}) copy-start(f32[2048]{0:T(1024)} %param.15) | copy-start | bytes 24580
Sparse Core Ops, SparseCore 0:
  19.3 35.7 reduce-scatter.1
  58.0 39.8 all-reduce.4
  101.9 55.4 all-reduce.6
where the time goes:
time: 218 us
  waiting for transfers between devices  113 us (52%)
  blocking collectives  62.6 us (29%)
  matrix products  21.3 us (10%)
  between operations  14.5 us (7%)
  other arithmetic  4.58 us (2%)
    unnamed x4, waiting for transfers between devices  55.5 us
    psum x1, waiting for transfers between devices, shards(): doc_total = lax.psum(feature_block, 'segment')  42.1 us
    unnamed x1, blocking collectives  18.2 us
    psum x1, blocking collectives, shards(): combined = lax.psum(head_terms, 'segment')  16.2 us
    reduce_scatter x1, waiting for transfers between devices, shards(): lax.psum_scatter(section_part, 'seq', scatter_dimension=1, tiled=True)  15.9 us
    all_gather x1, blocking collectives, shards(): lax.all_gather(keys_here, 'seq', axis=0, tiled=True)  14.1 us
    all_gather x1, blocking collectives, shards(): lax.all_gather(values_here, 'seq', axis=0, tiled=True)  14.1 us
    dot_general x1, matrix products, shards(): partial_value = jnp.dot(member, tokens, preferred_element_type=jnp.float32)  8.85 us
  transfers between devices with their start and end apart: 3, of which 3 were waited for; matrix products, arithmetic and copies ran while one was open for 1% of the time, Pallas kernels for 0%

commit v1 on v0

--- a/solution.py
+++ b/solution.py
@@ -36,7 +36,13 @@
     doc_onehot = (section_ids[:, None] == doc_sections[None, :]).astype(jnp.float32)
     section_part = jnp.dot(doc_onehot, weighted, precision=lax.Precision.HIGHEST)
     feature_block = lax.psum_scatter(section_part, "seq", scatter_dimension=1, tiled=True)
-    doc_total = lax.psum(feature_block, "segment")
+    peers = lax.axis_size("segment")
+    doc_total, reach = (feature_block, 1)
+    while reach < peers:
+        doc_total = doc_total + lax.ppermute(
+            doc_total, "segment", [(i, i ^ reach) for i in range(peers)]
+        )
+        reach = 2 * reach
     pooled = (doc_total / jnp.maximum(count_all, 1.0)[:, None]).astype(jnp.bfloat16)
     projected = jnp.dot(pooled, w_in, preferred_element_type=jnp.float32)
     section_in = lax.psum_scatter(projected, "seq", scatter_dimension=0, tiled=True)

time: 218 us -> 185 us (0.85)
  waiting for transfers between devices: 113 us -> 77.3 us
    psum x1 -> x0, waiting for transfers between devices: 42.1 us -> none  [shards(): doc_total = lax.psum(feature_block, 'segment')]
    ppermute x0 -> x2, waiting for transfers between devices: none -> 7.42 us  [shards(): lax.ppermute(doc_total, 'segment', [(i, i ^ reach) for i in range(peers)])]
    unnamed x4 -> x3, waiting for transfers between devices: 55.5 us -> 54 us
  transfers between devices with their start and end apart: 3 -> 4, of which waited for: 3 -> 4; matrix products, arithmetic and copies ran while one was open for 1% -> 1% of each run, Pallas kernels for 0% -> 0%
where the time goes in v1:
time: 185 us
  waiting for transfers between devices  77.3 us (42%)
  blocking collectives  62.6 us (34%)
  matrix products  21.3 us (12%)
  between operations  14.8 us (8%)
  other arithmetic  5.5 us (3%)
  starting transfers between devices  2.18 us (1%)
    unnamed x3, waiting for transfers between devices  54 us
    unnamed x1, blocking collectives  18.2 us
    psum x1, blocking collectives, shards(): combined = lax.psum(head_terms, 'segment')  16.2 us
    reduce_scatter x1, waiting for transfers between devices, shards(): lax.psum_scatter(section_part, 'seq', scatter_dimension=1, tiled=True)  15.9 us
    all_gather x1, blocking collectives, shards(): lax.all_gather(keys_here, 'seq', axis=0, tiled=True)  14.1 us
    all_gather x1, blocking collectives, shards(): lax.all_gather(values_here, 'seq', axis=0, tiled=True)  14.1 us
    dot_general x1, matrix products, shards(): partial_value = jnp.dot(member, tokens, preferred_element_type=jnp.float32)  8.85 us
    ppermute x2, waiting for transfers between devices, shards(): lax.ppermute(doc_total, 'segment', [(i, i ^ reach) for i in range(peers)])  7.42 us
  transfers between devices with their start and end apart: 4, of which 4 were waited for; matrix products, arithmetic and copies ran while one was open for 1% of the time, Pallas kernels for 0%

profile of v1, /device:TPU:0, one launch (start us, length us, event | category | flops | bytes accessed | tf_op | source)
XLA Modules:
  0.0 184.8 jit_solution(5131011088343930283)
XLA Ops:
  6.5 0.9 fusion.30
  7.7 0.7 bitcast_subtract_fusion
  8.4 8.8 %fusion.3 = f32[64,8192]{1,0:T(8,128)S(1)} fusion(bf16[1,1024,8192]{2,1,0:T(8,128)(2,1)} %param.10, f32[64]{0:T(128)S(1)} %get-tuple-element.6, s32[1024]{0:T(1024)S(1)} %iota_add_fusion, s32[64]{0:T(128)S(1)} %reduce, s32[64]{0:T(128)S(1)} %bitcast_subtract_fusion), kind=kOutput, calls=%fused_computation.3 | convolution fusion | flops 1074462720 | bytes 18879232 | tf_op jit(solution)/shard_map/dot_general | solution.py:24
  17.3 1.8 fusion.25
  19.3 0.7 fusion.31
  20.6 0.2 dynamic-update-slice
  20.9 18.2 %all-reduce = bf16[32]{0:T(256)(128)(2,1)S(1)} all-reduce(bf16[32]{0:T(256)(128)(2,1)S(1)} %dynamic-update-slice), channel_id=1, replica_groups=mesh['segment'=4,'seq'=8] {'seq'}, use_global_device_ids=true, to_apply=%add | all-reduce | flops 32 | bytes 128
  39.2 15.9 %reduce-scatter.2.cloned.1.call-done = f32[32,1024]{1,0:T(8,128)} async-done(((f32[32,8192]{1,0:T(8,128)}), f32[32,1024]{1,0:T(8,128)}) %reduce-scatter.2.cloned.1.call-update) | async-done | bytes 131088 | tf_op jit(solution)/shard_map/reduce_scatter | solution.py:38
  55.1 1.0 collective-permute-start
  56.1 4.1 %collective-permute-done = f32[32,1024]{1,0:T(8,128)S(1)} collective-permute-done((f32[32,1024]{1,0:T(8,128)}, f32[32,1024]{1,0:T(8,128)S(1)}, u32[]{:S(2)}, u32[]{:S(2)}) %collective-permute-start) | collective-permute-done | bytes 131104 | tf_op jit(solution)/shard_map/ppermute | solution.py:42
  60.3 0.9 add.51
  61.2 1.1 collective-permute-start.1
  62.9 3.3 %collective-permute-done.1 = f32[32,1024]{1,0:T(8,128)S(1)} collective-permute-done((f32[32,1024]{1,0:T(8,128)S(1)}, f32[32,1024]{1,0:T(8,128)S(1)}, u32[]{:S(2)}, u32[]{:S(2)}) %collective-permute-start.1) | collective-permute-done | bytes 131104 | tf_op jit(solution)/shard_map/ppermute | solution.py:42
  66.2 3.8 %fusion.20 = f32[32,2048]{1,0:T(8,128)} fusion(bf16[1024,2048]{1,0:T(8,128)(2,1)} %param.14, f32[32,1024]{1,0:T(8,128)S(1)} %add.51, f32[32,1024]{1,0:T(8,128)S(1)} %collective-permute-done.1, f32[32]{0:T(128)S(1)} %broadcast_maximum_fusion), kind=kOutput, calls=%fused_computation.24 | convolution fusion | flops 134316032 | bytes 4718720 | tf_op jit(solution)/shard_map/dot_general | solution.py:47
  70.1 54.0 %all-reduce.4.cloned.1.call-done = f32[32,2048]{1,0:T(8,128)} async-done(((f32[32,2048]{1,0:T(8,128)}), f32[32,2048]{1,0:T(8,128)}) %all-reduce.4.cloned.1.call-update) | async-done | bytes 262160
  124.1 1.0 multiply_reduce_fusion
  125.1 2.0 %fusion.11 = bf16[1,4,512]{2,1,0:T(4,128)(2,1)S(1)} fusion(bf16[2048,512]{1,0:T(8,128)(2,1)} %param.17, f32[32,2048]{1,0:T(8,128)} %all-reduce.4.cloned.1.call-done, u32[]{:T(128)S(6)} %multiply.11, f32[2048]{0:T(1024)S(1)} %copy-done.1, f32[4]{0:T(128)S(1)} %add_rsqrt_fusion), kind=kOutput, calls=%fused_computation.14 | convolution fusion | flops 8415232 | bytes 2142228 | tf_op jit(solution)/shard_map/dot_general | solution.py:52
  127.1 14.1 %all-gather.1 = bf16[8,4,512]{2,1,0:T(4,128)(2,1)S(1)} all-gather(bf16[1,4,512]{2,1,0:T(4,128)(2,1)S(1)} %fusion.11), channel_id=1, replica_groups=mesh['segment'=4,'seq'=8] {'seq'}, dimensions={0}, use_global_device_ids=true | all-gather | bytes 36864 | tf_op jit(solution)/shard_map/all_gather | solution.py:56
  141.2 2.2 %fusion.8 = f32[4,4,32]{2,1,0:T(4,128)S(1)} fusion(bf16[2048,512]{1,0:T(8,128)(2,1)} %param.16, bf16[32,4,128]{2,1,0:T(4,128)(2,1)S(1)} %reshape.108, pred[4,32]{1,0:T(4,128)(4,1)S(1)} %fusion.29, f32[32,2048]{1,0:T(8,128)} %all-reduce.4.cloned.1.call-done, u32[]{:T(128)S(6)} %multiply.11, f32[2048]{0:T(1024)S(1)} %copy-done.1, f32[4]{0:T(128)S(1)} %add_rsqrt_fusion), kind=kOutput, calls=%fused_computation.7 | convolution fusion | flops 8547328 | bytes 2173076 | tf_op jit(solution)/shard_map/qhd,khd->hqk/dot_general | solution.py:64
  143.5 2.1 %fusion.9 = bf16[1,4,512]{2,1,0:T(4,128)(2,1)S(1)} fusion(bf16[2048,512]{1,0:T(8,128)(2,1)} %param.18, f32[32,2048]{1,0:T(8,128)} %all-reduce.4.cloned.1.call-done, u32[]{:T(128)S(6)} %multiply.11, f32[2048]{0:T(1024)S(1)} %copy-done.1, f32[4]{0:T(128)S(1)} %add_rsqrt_fusion), kind=kOutput, calls=%fused_computation.12 | convolution fusion | flops 8415232 | bytes 2142228 | tf_op jit(solution)/shard_map/dot_general | solution.py:53
  145.6 14.1 %all-gather = bf16[8,4,512]{2,1,0:T(4,128)(2,1)S(1)} all-gather(bf16[1,4,512]{2,1,0:T(4,128)(2,1)S(1)} %fusion.9), channel_id=1, replica_groups=mesh['segment'=4,'seq'=8] {'seq'}, dimensions={0}, use_global_device_ids=true | all-gather | bytes 36864 | tf_op jit(solution)/shard_map/all_gather | solution.py:57
  159.7 0.5 fusion.13
  160.3 16.2 %psum.7 = f32[4,2048]{1,0:T(4,128)S(1)} all-reduce(f32[4,2048]{1,0:T(4,128)S(1)} %fusion.13), channel_id=1, replica_groups=mesh['segment'=4,'seq'=8] {'segment'}, use_global_device_ids=true, to_apply=%region_7.8 | all-reduce | flops 8192 | bytes 65536 | tf_op jit(solution)/shard_map/psum | solution.py:74
  176.5 1.5 add_convert_fusion
  (30 shorter events, 0.9 us)
Async XLA Ops:
  6.5 153.2 %copy-start = (bf16[512,2048]{1,0:T(8,128)(2,1)S(1)}, bf16[512,2048]{1,0:T(8,128)(2,1)}, u32[]{:S(2)}) copy-start(bf16[512,2048]{1,0:T(8,128)(2,1)} %param.19) | copy-start | bytes 6291460
  6.5 48.5 %reduce-scatter.2.cloned.1.call-start = ((), (), s32[]{:S(2)}) async-start(), calls=%async_computation.1 | async-start | bytes 1179648 | tf_op jit(solution)/shard_map/reduce_scatter | solution.py:38
  17.3 1.9 %copy-start.2 = (s32[4,64]{1,0:T(4,128)S(1)}, s32[4,64]{1,0:T(4,128)}, u32[]{:S(2)}) copy-start(s32[4,64]{1,0:T(4,128)} %param.12) | copy-start | bytes 3076
  17.3 2.0 %copy-start.4 = (s32[4]{0:T(128)S(1)}, s32[4]{0:T(128)}, u32[]{:S(2)}) copy-start(s32[4]{0:T(128)} %param.13) | copy-start | bytes 52
  17.3 2.0 %copy-start.3 = (u32[32]{0:T(128)S(1)}, u32[32]{0:T(128)}, u32[]{:S(2)}) copy-start(u32[32]{0:T(128)} %constant.45) | copy-start | bytes 388
  19.1 104.9 %all-reduce.4.cloned.1.call-start = ((), (), s32[]{:S(2)}) async-start(), calls=%async_computation.2 | async-start | bytes 524288
  55.1 5.2 %collective-permute-start = (f32[32,1024]{1,0:T(8,128)}, f32[32,1024]{1,0:T(8,128)S(1)}, u32[]{:S(2)}, u32[]{:S(2)}) collective-permute-start(f32[32,1024]{1,0:T(8,128)} %reduce-scatter.2.cloned.1.call-done), channel_id=1, source_target_pairs={{0,8},{8,0},{16,24},{24,16},{1,9},{9,1},{17,25},{25,17},{2,10},{10... | collective-permute-start | bytes 393224 | tf_op jit(solution)/shard_map/ppermute | solution.py:42
  61.2 5.0 %collective-permute-start.1 = (f32[32,1024]{1,0:T(8,128)S(1)}, f32[32,1024]{1,0:T(8,128)S(1)}, u32[]{:S(2)}, u32[]{:S(2)}) collective-permute-start(f32[32,1024]{1,0:T(8,128)S(1)} %add.51), channel_id=1, source_target_pairs={{0,16},{8,24},{16,0},{24,8},{1,17},{9,25},{17,1},{25,9},{2,18},{10... | collective-permute-start | bytes 393224 | tf_op jit(solution)/shard_map/ppermute | solution.py:42
  62.9 62.1 %copy-start.1 = (f32[2048]{0:T(1024)S(1)}, f32[2048]{0:T(1024)}, u32[]{:S(2)}) copy-start(f32[2048]{0:T(1024)} %param.15) | copy-start | bytes 24580
Sparse Core Ops, SparseCore 0:
  19.3 35.7 reduce-scatter.1
  70.1 53.8 all-reduce.3
